TPU v7x, 256 devices: a whole 4x4x8 slice. The times are simulated.
256 devices in a mesh: read: 32 (over z_lo, x, core), pos: 8 (over y, z_hi).
Axes of the slice: x: 4, y: 4, z: 8 (z_hi: 2, z_lo: 4; z = z_hi * 4 + z_lo), core: 2. Of those that a mesh axis runs over, the one named last changes fastest.
Arguments:
- features: bfloat16 [128, 256, 768], P('read', 'pos'), may hold values from -6 to 6
- grad_out: bfloat16 [128, 256, 768], P('read', 'pos'), may hold values from -16 to 16
- weights: bfloat16 [4, 768, 768], replicated, may hold values from -0.21875 to 0.21875
- read_start: int32 [128], replicated, may hold values from 0 to 127
- read_end: int32 [128], replicated, may hold values from 129 to 256
Outputs:
- grad_input: bfloat16 [128, 256, 768], P('read', 'pos')
- weight_grads: float32 [768, 3072], P(('read', 'pos'))
Inputs may be any that keep to these rules, and one draw needn't show every extreme that they name: read_end is above read_start for every read.
All inputs are finite; a program needn't handle non-finite values.
Results may differ from a plain program's by a relative error of at most 0.0086.
Values may be sent and summed in bfloat16 or wider, within the bound.
A program may use at most 128 MiB of HBM per device.

v0:
```python
import math
import jax
import jax.numpy as jnp
from jax import lax
from jax.sharding import PartitionSpec as P

HEADS = 12
HEAD_DIM = 64


def coverage(starts, ends, first_col, col_count):
    columns = first_col + jnp.arange(col_count, dtype=jnp.int32)
    inside = (columns[None, :] >= starts[:, None]) & (columns[None, :] < ends[:, None])
    return inside.astype(jnp.float32)


def dot_back(left, right):
    return lax.dot_general(
        left, right, (((1,), (1,)), ((), ())), preferred_element_type=jnp.float32
    )


def project(source, upstream, covered, weights):
    width = source.shape[-1]
    values32 = source.reshape(-1, width).astype(jnp.float32)
    inverse = lax.rsqrt(jnp.mean(values32 * values32, -1, keepdims=True) + 1e-05)
    normed = values32 * inverse
    normed_b = normed.astype(jnp.bfloat16)
    keep_mask = covered.reshape(-1, 1)
    query = (jnp.dot(normed_b, weights[0], preferred_element_type=jnp.float32) * keep_mask).astype(
        jnp.bfloat16
    )
    keys = (jnp.dot(normed_b, weights[1], preferred_element_type=jnp.float32) * keep_mask).astype(
        jnp.bfloat16
    )
    values = (jnp.dot(normed_b, weights[2], preferred_element_type=jnp.float32) * keep_mask).astype(
        jnp.bfloat16
    )
    grad_flat = upstream.reshape(-1, width)
    back_out = dot_back(grad_flat, weights[3]).astype(jnp.bfloat16)
    return (normed, inverse, normed_b, grad_flat, query, keys, values, back_out)


def attend(query, keys, values, back_out, covered, scale):
    reads, narrow, width = query.shape
    shape4 = (reads, narrow, HEADS, HEAD_DIM)
    query4 = query.reshape(shape4)
    keys4 = keys.reshape(shape4)
    values4 = values.reshape(shape4)
    back4 = back_out.reshape(shape4)
    partial_logits = jnp.einsum("rchd,schd->hrs", query4, keys4, preferred_element_type=jnp.float32)
    logits = lax.psum(partial_logits, ("read", "pos")) * scale
    expon = jnp.exp(logits)
    probs = expon / jnp.sum(expon, -1, keepdims=True)
    probs_b = probs.astype(jnp.bfloat16)
    slopes = lax.psum(
        jnp.einsum("rchd,schd->hrs", back4, values4, preferred_element_type=jnp.float32),
        ("read", "pos"),
    )
    mixed = (scale * probs * (slopes - jnp.sum(probs * slopes, -1, keepdims=True))).astype(
        jnp.bfloat16
    )
    output = jnp.einsum(
        "hrs,schd->rchd", probs_b, values4, preferred_element_type=jnp.float32
    ).astype(jnp.bfloat16)
    keep4 = covered[:, :, None, None]
    grad_query = (
        jnp.einsum("hrs,schd->rchd", mixed, keys4, preferred_element_type=jnp.float32) * keep4
    ).astype(jnp.bfloat16)
    grad_keys = (
        jnp.einsum("hrs,rchd->schd", mixed, query4, preferred_element_type=jnp.float32) * keep4
    ).astype(jnp.bfloat16)
    grad_values = (
        jnp.einsum("hrs,rchd->schd", probs_b, back4, preferred_element_type=jnp.float32) * keep4
    ).astype(jnp.bfloat16)
    shape3 = (reads, narrow, width)
    return (
        output.reshape(shape3),
        grad_query.reshape(shape3),
        grad_keys.reshape(shape3),
        grad_values.reshape(shape3),
    )


def input_grad(grad_query, grad_keys, grad_values, weights, normed, inverse):
    grad_norm = (
        dot_back(grad_query, weights[0])
        + dot_back(grad_keys, weights[1])
        + dot_back(grad_values, weights[2])
    )
    result = inverse * (grad_norm - normed * jnp.mean(grad_norm * normed, -1, keepdims=True))
    return result.astype(jnp.bfloat16)


def shards(features, grad_out, weights, read_start, read_end):
    rows, col_dev, width = features.shape
    read_count = lax.axis_size("read")
    pos_count = lax.axis_size("pos")
    read_at = lax.axis_index("read")
    pos_at = lax.axis_index("pos")
    scale = 1.0 / math.sqrt(HEAD_DIM * col_dev * pos_count)
    narrow = col_dev // read_count
    column_first = pos_at * col_dev + read_at * narrow
    column_cover = coverage(read_start, read_end, column_first, narrow)
    starts = lax.dynamic_slice_in_dim(read_start, read_at * rows, rows)
    ends = lax.dynamic_slice_in_dim(read_end, read_at * rows, rows)
    covered = coverage(starts, ends, pos_at * col_dev, col_dev)
    normed, inverse, normed_b, grad_flat, query, keys, values, back_out = project(
        features, grad_out, covered, weights
    )
    token_shape = (rows, col_dev, width)
    col_query, col_keys, col_values, col_back = (
        lax.all_to_all(query.reshape(token_shape), "read", split_axis=1, concat_axis=0, tiled=True),
        lax.all_to_all(keys.reshape(token_shape), "read", split_axis=1, concat_axis=0, tiled=True),
        lax.all_to_all(
            values.reshape(token_shape), "read", split_axis=1, concat_axis=0, tiled=True
        ),
        lax.all_to_all(
            back_out.reshape(token_shape), "read", split_axis=1, concat_axis=0, tiled=True
        ),
    )
    output, grad_query, grad_keys, grad_values = attend(
        col_query, col_keys, col_values, col_back, column_cover, scale
    )
    output, grad_query, grad_keys, grad_values = (
        lax.all_to_all(output, "read", split_axis=0, concat_axis=1, tiled=True),
        lax.all_to_all(grad_query, "read", split_axis=0, concat_axis=1, tiled=True),
        lax.all_to_all(grad_keys, "read", split_axis=0, concat_axis=1, tiled=True),
        lax.all_to_all(grad_values, "read", split_axis=0, concat_axis=1, tiled=True),
    )
    output_flat = output.reshape(-1, width)
    query_flat = grad_query.reshape(-1, width)
    keys_flat = grad_keys.reshape(-1, width)
    values_flat = grad_values.reshape(-1, width)
    grad_input = input_grad(query_flat, keys_flat, values_flat, weights, normed, inverse).reshape(
        token_shape
    )
    right_side = jnp.concatenate([query_flat, keys_flat, values_flat], axis=1)
    inner_part = lax.dot_general(
        normed_b, right_side, (((0,), (0,)), ((), ())), preferred_element_type=jnp.float32
    )
    outer_part = lax.dot_general(
        output_flat, grad_flat, (((0,), (0,)), ((), ())), preferred_element_type=jnp.float32
    )
    weight_grads = lax.psum_scatter(
        jnp.concatenate([inner_part, outer_part], axis=1),
        ("read", "pos"),
        scatter_dimension=0,
        tiled=True,
    )
    return (grad_input, weight_grads)


def solution(mesh):
    in_specs = (P("read", "pos", None), P("read", "pos", None), P(), P(), P())
    out_specs = (P("read", "pos", None), P(("read", "pos"), None))
    return jax.shard_map(shards, mesh=mesh, in_specs=in_specs, out_specs=out_specs, check_vma=False)
```

profile of v0, /device:TPU:97, one launch (start us, length us, event | category | flops | bytes accessed | tf_op | source)
XLA Modules:
  0.0 704.0 jit_solution(4038250459228061290)
XLA Ops:
  7.2 1.1 multiply_reduce_fusion.2
  8.3 1.0 multiply_convert_fusion.2
  9.3 0.7 dynamic_slice.7
  10.1 0.7 dynamic_slice.6
  11.0 1.6 fusion.16
  12.6 0.8 copy.33
  13.4 8.0 %all-to-all-start = ((bf16[4,32,768]{2,0,1:T(4,128)(2,1)}), bf16[4,32,768]{2,0,1:T(4,128)(2,1)S(1)}, u32[]{:S(2)}, u32[]{:S(2)}) async-start(bf16[4,32,768]{2,0,1:T(4,128)(2,1)} %copy.33), calls=%async_computation | async-start | bytes 393216 | tf_op jit(solution)/shard_map/all_to_all | solution.py:114
  21.5 1.8 fusion.13
  23.3 0.8 copy.37
  24.1 5.1 all-to-all-done
  29.2 5.8 all-to-all-start.2
  35.0 1.6 fusion.22
  36.6 0.8 copy.38
  37.4 5.3 all-to-all-done.2
  42.7 5.8 all-to-all-start.3
  48.5 1.6 fusion.19
  50.1 0.8 copy.34
  50.9 5.3 all-to-all-done.3
  56.3 5.8 all-to-all-start.1
  62.4 0.4 copy.41
  63.1 0.4 copy.39
  63.8 0.4 copy.40
  64.2 5.6 all-to-all-done.1
  70.1 0.4 copy.35
  70.5 1.2 fusion.49
  71.7 1.2 fusion.48
  73.0 263.2 %all-reduce.7.cloned.1.call-done = (f32[12,128,128]{2,1,0:T(8,128)}, f32[12,128,128]{2,1,0:T(8,128)}) async-done(((f32[12,128,128]{2,1,0:T(8,128)}, f32[12,128,128]{2,1,0:T(8,128)}), (f32[12,128,128]{2,1,0:T(8,128)}, f32[12,128,128]{2,1,0:T(8,128)})) %all-reduce.7.cloned.1.call-update) | async-done | bytes 1572880 | tf_op jit(solution)/shard_map/psum | solution.py:56
  336.2 1.5 fusion.35
  337.7 1.9 multiply_reduce_fusion
  339.6 1.8 multiply_convert_fusion
  341.4 0.4 fusion.27
  341.8 0.5 broadcast.84
  342.3 0.8 reduce.5
  343.2 0.8 reshape.206
  344.0 7.4 %all-to-all-start.4 = ((bf16[32,2,1536]{2,1,0:T(2,128)(2,1)}), bf16[32,2,1536]{2,1,0:T(2,128)(2,1)S(1)}, u32[]{:S(2)}, u32[]{:S(2)}) async-start(bf16[32,2,1536]{2,1,0:T(2,128)(2,1)} %reshape.206), calls=%async_computation.4 | async-start | bytes 393216 | tf_op jit(solution)/shard_map/all_to_all | solution.py:127
  351.7 0.8 reduce.6
  352.6 0.8 reshape.208
  353.4 5.8 all-to-all-done.4
  359.2 5.8 all-to-all-start.5
  365.0 0.5 fusion.25
  365.5 0.8 reduce.7
  366.4 0.8 reshape.210
  367.2 5.6 all-to-all-done.5
  372.8 5.8 all-to-all-start.6
  378.5 0.5 convolution_convert_fusion
  379.0 0.8 reduce.8
  379.9 0.8 reshape.212
  380.7 5.6 all-to-all-done.6
  386.3 5.8 all-to-all-start.7
  392.4 1.2 reduce.1
  393.8 1.2 reduce.2
  395.2 1.2 reduce.3
  396.4 2.6 fusion.7
  399.0 0.9 all-to-all-done.7
  400.0 1.2 reduce.4
  401.2 0.5 fusion.50
  401.7 1.9 convolution_add_fusion.1
  403.6 2.6 fusion.42
  406.2 3.9 fusion.36
  410.2 8.1 %pad_maximum_fusion = f32[768,3072]{1,0:T(8,128)} fusion(f32[768,768]{1,0:T(8,128)S(1)} %fusion.50, f32[768,2304]{1,0:T(8,128)} %fusion.36), kind=kLoop, calls=%fused_computation | loop fusion | flops 2359296 | bytes 18874368 | tf_op jit(solution)/shard_map/concatenate | solution.py:146
  418.3 1.0 copy-done.3
  419.2 0.9 multiply_convert_fusion.1
  420.1 275.6 %all-reduce.5.cloned.1.call-done = f32[768,3072]{1,0:T(8,128)} async-done(((f32[768,3072]{1,0:T(8,128)}), f32[768,3072]{1,0:T(8,128)}) %all-reduce.5.cloned.1.call-update) | async-done | bytes 9437200
  695.6 1.6 constant_dynamic-slice_fusion
  (43 shorter events, 3.3 us)
Async XLA Ops:
  7.2 14.3 %copy-start = (bf16[4,32,768]{2,1,0:T(8,128)(2,1)S(1)}, bf16[4,32,768]{2,1,0:T(8,128)(2,1)}, u32[]{:S(2)}) copy-start(bf16[4,32,768]{2,1,0:T(8,128)(2,1)} %param.6) | copy-start | bytes 589828
  13.4 15.8 %all-to-all-start = ((bf16[4,32,768]{2,0,1:T(4,128)(2,1)}), bf16[4,32,768]{2,0,1:T(4,128)(2,1)S(1)}, u32[]{:S(2)}, u32[]{:S(2)}) async-start(bf16[4,32,768]{2,0,1:T(4,128)(2,1)} %copy.33), calls=%async_computation | async-start | bytes 393216 | tf_op jit(solution)/shard_map/all_to_all | solution.py:114
  29.2 13.5 %all-to-all-start.2 = ((bf16[4,32,768]{2,0,1:T(4,128)(2,1)}), bf16[4,32,768]{2,0,1:T(4,128)(2,1)S(1)}, u32[]{:S(2)}, u32[]{:S(2)}) async-start(bf16[4,32,768]{2,0,1:T(4,128)(2,1)} %copy.37), calls=%async_computation.2 | async-start | bytes 393216 | tf_op jit(solution)/shard_map/all_to_all | solution.py:118
  42.7 13.5 %all-to-all-start.3 = ((bf16[4,32,768]{2,0,1:T(4,128)(2,1)}), bf16[4,32,768]{2,0,1:T(4,128)(2,1)S(1)}, u32[]{:S(2)}, u32[]{:S(2)}) async-start(bf16[4,32,768]{2,0,1:T(4,128)(2,1)} %copy.38), calls=%async_computation.3 | async-start | bytes 393216 | tf_op jit(solution)/shard_map/all_to_all | solution.py:115
  56.3 13.5 %all-to-all-start.1 = ((bf16[4,32,768]{2,0,1:T(4,128)(2,1)}), bf16[4,32,768]{2,0,1:T(4,128)(2,1)S(1)}, u32[]{:S(2)}, u32[]{:S(2)}) async-start(bf16[4,32,768]{2,0,1:T(4,128)(2,1)} %copy.34), calls=%async_computation.1 | async-start | bytes 393216 | tf_op jit(solution)/shard_map/all_to_all | solution.py:113
  62.0 274.1 %all-reduce.7.cloned.1.call-start = ((), (), s32[]{:S(2)}) async-start(), calls=%async_computation.9 | async-start | bytes 3145728 | tf_op jit(solution)/shard_map/psum | solution.py:56
  62.1 10.9 %copy-start.4 = (s32[128]{0:T(128)S(1)}, s32[128]{0:T(128)}, u32[]{:S(2)}) copy-start(s32[128]{0:T(128)} %param.9) | copy-start | bytes 1540
  62.1 10.9 %copy-start.5 = (s32[128]{0:T(128)S(1)}, s32[128]{0:T(128)}, u32[]{:S(2)}) copy-start(s32[128]{0:T(128)} %param.8) | copy-start | bytes 1540
  336.2 28.8 %copy-start.1 = (f32[12,128,128]{2,1,0:T(8,128)S(1)}, f32[12,128,128]{2,1,0:T(8,128)}, u32[]{:S(2)}) copy-start(f32[12,128,128]{2,1,0:T(8,128)} %get-tuple-element.3) | copy-start | bytes 2359300
  344.0 15.2 %all-to-all-start.4 = ((bf16[32,2,1536]{2,1,0:T(2,128)(2,1)}), bf16[32,2,1536]{2,1,0:T(2,128)(2,1)S(1)}, u32[]{:S(2)}, u32[]{:S(2)}) async-start(bf16[32,2,1536]{2,1,0:T(2,128)(2,1)} %reshape.206), calls=%async_computation.4 | async-start | bytes 393216 | tf_op jit(solution)/shard_map/all_to_all | solution.py:127
  359.2 13.5 %all-to-all-start.5 = ((bf16[32,2,1536]{2,1,0:T(2,128)(2,1)}), bf16[32,2,1536]{2,1,0:T(2,128)(2,1)S(1)}, u32[]{:S(2)}, u32[]{:S(2)}) async-start(bf16[32,2,1536]{2,1,0:T(2,128)(2,1)} %reshape.208), calls=%async_computation.5 | async-start | bytes 393216 | tf_op jit(solution)/shard_map/all_to_all | solution.py:128
  372.8 13.5 %all-to-all-start.6 = ((bf16[32,2,1536]{2,1,0:T(2,128)(2,1)}), bf16[32,2,1536]{2,1,0:T(2,128)(2,1)S(1)}, u32[]{:S(2)}, u32[]{:S(2)}) async-start(bf16[32,2,1536]{2,1,0:T(2,128)(2,1)} %reshape.210), calls=%async_computation.6 | async-start | bytes 393216 | tf_op jit(solution)/shard_map/all_to_all | solution.py:129
  386.3 13.5 %all-to-all-start.7 = ((bf16[32,2,1536]{2,1,0:T(2,128)(2,1)}), bf16[32,2,1536]{2,1,0:T(2,128)(2,1)S(1)}, u32[]{:S(2)}, u32[]{:S(2)}) async-start(bf16[32,2,1536]{2,1,0:T(2,128)(2,1)} %reshape.212), calls=%async_computation.7 | async-start | bytes 393216 | tf_op jit(solution)/shard_map/all_to_all | solution.py:126
  392.1 303.6 %all-reduce.5.cloned.1.call-start = ((), (), s32[]{:S(2)}) async-start(), calls=%async_computation.8 | async-start | bytes 18874368
  396.3 7.3 %copy-start.2 = (bf16[4,32,768]{2,1,0:T(8,128)(2,1)S(1)}, bf16[4,32,768]{2,1,0:T(8,128)(2,1)}, u32[]{:S(2)}) copy-start(bf16[4,32,768]{2,1,0:T(8,128)(2,1)} %param.5) | copy-start | bytes 589828
  418.2 1.0 copy-start.3
Sparse Core Ops, SparseCore 0:
  73.1 263.0 all-reduce.6
  418.4 277.2 all-reduce.4
where the time goes:
time: 705 us; the launch traced here: 704 us
  waiting for transfers between devices  578 us (82%)
  starting transfers between devices  50.2 us (7%)
  other arithmetic  24 us (3%)
  matrix products  22 us (3%)
  local copies, waits for them, and re-layouts  15.4 us (2%)
  between operations  14.5 us (2%)
    unnamed x3, waiting for transfers between devices  276 us
    psum x1, waiting for transfers between devices, attend(): lax.psum(jnp.einsum('rchd,schd->hrs', back4, values4, preferred_element_t...  263 us
  transfers between devices with their start and end apart: 10, of which 10 were waited for; matrix products, arithmetic and copies ran while one was open for 3% of the time, Pallas kernels for 0%

commit v1 on v0

--- a/solution.py
+++ b/solution.py
@@ -54,8 +54,10 @@
     probs = expon / jnp.sum(expon, -1, keepdims=True)
     probs_b = probs.astype(jnp.bfloat16)
     slopes = lax.psum(
-        jnp.einsum("rchd,schd->hrs", back4, values4, preferred_element_type=jnp.float32),
-        ("read", "pos"),
+        lax.psum(
+            jnp.einsum("rchd,schd->hrs", back4, values4, preferred_element_type=jnp.float32), "pos"
+        ),
+        "read",
     )
     mixed = (scale * probs * (slopes - jnp.sum(probs * slopes, -1, keepdims=True))).astype(
         jnp.bfloat16

time: 705 us -> 1070 us (1.52)
  waiting for transfers between devices: 578 us -> 923 us
  starting transfers between devices: 50.2 us -> 66.2 us
    psum x0 -> x2, waiting for transfers between devices: none -> 522 us  [the longest x1 270 us: attend(): logits = lax.psum(partial_logits, ('read', 'pos')) * scale]
    psum x1, waiting for transfers between devices: 263 us -> 92.8 us  [attend(): lax.psum(jnp.einsum('rchd,schd->hrs', back4, values4, preferred_element_t...]
    all_to_all x1, starting transfers between devices: 5.76 us -> 20.8 us  [shards(): lax.all_to_all(output, 'read', split_axis=0, concat_axis=1, tiled=True)]
    unnamed x3 -> x5, waiting for transfers between devices: 276 us -> 279 us
  transfers between devices with their start and end apart: 10 -> 12, of which waited for: 10 -> 11; matrix products, arithmetic and copies ran while one was open for 3% -> 4% of each run, Pallas kernels for 0% -> 0%
where the time goes in v1:
time: 1070 us
  waiting for transfers between devices  923 us (86%)
  starting transfers between devices  66.2 us (6%)
  other arithmetic  24.1 us (2%)
  matrix products  22.5 us (2%)
  local copies, waits for them, and re-layouts  17.7 us (2%)
  between operations  14.2 us (1%)
    unnamed x5, waiting for transfers between devices  279 us
    psum x1, waiting for transfers between devices, attend(): logits = lax.psum(partial_logits, ('read', 'pos')) * scale  270 us
    psum x1, waiting for transfers between devices, attend(): lax.psum(lax.psum(jnp.einsum('rchd,schd->hrs', back4, values4, preferred_...  252 us
    psum x1, waiting for transfers between devices, attend(): lax.psum(jnp.einsum('rchd,schd->hrs', back4, values4, preferred_element_t...  92.8 us
  transfers between devices with their start and end apart: 12, of which 11 were waited for; matrix products, arithmetic and copies ran while one was open for 4% of the time, Pallas kernels for 0%

profile of v1, /device:TPU:97, one launch (start us, length us, event | category | flops | bytes accessed | tf_op | source)
XLA Modules:
  0.0 1068.0 jit_solution(5765818076839455438)
XLA Ops:
  7.2 0.9 copy-done
  8.1 1.8 fusion.13
  9.9 0.8 copy.37
  10.7 8.1 all-to-all-start.2
  18.8 1.0 multiply_reduce_fusion.2
  19.9 1.0 multiply_convert_fusion.2
  20.9 0.7 dynamic_slice.7
  21.7 0.7 dynamic_slice.6
  22.5 1.6 fusion.22
  24.1 0.8 copy.38
  25.0 1.6 all-to-all-done.2
  26.6 6.1 all-to-all-start.3
  32.7 1.6 fusion.16
  34.3 0.8 copy.33
  35.5 0.4 copy.39
  35.8 4.6 all-to-all-done.3
  40.5 5.8 all-to-all-start
  46.6 0.4 copy.40
  47.0 1.2 fusion.49
  48.2 1.6 fusion.19
  49.9 0.8 copy.34
  50.7 3.3 all-to-all-done
  54.0 5.8 all-to-all-start.1
  60.5 10.1 all-to-all-done.1
  71.3 1.2 fusion.48
  72.6 92.8 %all-reduce.8.cloned.1.call-done = f32[12,128,128]{2,1,0:T(8,128)} async-done(((f32[12,128,128]{2,1,0:T(8,128)}), f32[12,128,128]{2,1,0:T(8,128)}) %all-reduce.8.cloned.1.call-update) | async-done | bytes 786448 | tf_op jit(solution)/shard_map/psum | solution.py:57
  165.4 269.7 %all-reduce.6.cloned.1.call-done = f32[12,128,128]{2,1,0:T(8,128)} async-done(((f32[12,128,128]{2,1,0:T(8,128)}), f32[12,128,128]{2,1,0:T(8,128)}) %all-reduce.6.cloned.1.call-update) | async-done | bytes 786448 | tf_op jit(solution)/shard_map/psum | solution.py:52
  435.1 1.5 fusion.35
  436.6 1.6 fusion.25
  438.2 0.5 broadcast.84
  438.7 0.8 reduce.7
  439.6 0.8 reshape.210
  440.4 7.4 all-to-all-start.6
  447.9 0.5 convolution_convert_fusion
  448.3 0.8 reduce.8
  449.3 0.8 reshape.212
  450.1 251.9 %all-reduce.10.cloned.1.call-done = f32[12,128,128]{2,1,0:T(8,128)} async-done(((f32[12,128,128]{2,1,0:T(8,128)}), f32[12,128,128]{2,1,0:T(8,128)}) %all-reduce.10.cloned.1.call-update) | async-done | bytes 786448 | tf_op jit(solution)/shard_map/psum | solution.py:56
  702.0 1.6 multiply_reduce_fusion
  703.6 20.8 %all-to-all-start.7 = ((bf16[32,2,1536]{2,1,0:T(2,128)(2,1)}), bf16[32,2,1536]{2,1,0:T(2,128)(2,1)S(1)}, u32[]{:S(2)}, u32[]{:S(2)}) async-start(bf16[32,2,1536]{2,1,0:T(2,128)(2,1)} %reshape.212), calls=%async_computation.7 | async-start | bytes 393216 | tf_op jit(solution)/shard_map/all_to_all | solution.py:128
  724.4 1.6 multiply_convert_fusion
  726.4 0.8 reduce.5
  727.3 0.8 reshape.206
  728.1 4.1 all-to-all-done.7
  732.2 5.8 all-to-all-start.4
  738.2 1.2 reduce.4
  739.7 0.8 reduce.6
  740.6 0.8 reshape.208
  741.4 4.3 all-to-all-done.4
  745.7 6.3 all-to-all-start.5
  752.1 0.5 fusion.50
  752.8 1.2 reduce.3
  754.2 1.2 reduce.1
  755.4 2.6 fusion.7
  758.0 1.8 all-to-all-done.5
  759.8 1.6 reshape.209
  761.4 1.8 reduce.2
  763.2 1.0 all_to_all.104
  764.2 1.9 convolution_add_fusion.1
  766.1 1.9 fusion.42
  768.1 4.0 fusion.36
  772.0 8.1 pad_maximum_fusion
  780.1 0.9 multiply_convert_fusion.1
  781.0 278.9 %all-reduce.12.cloned.1.call-done = f32[768,3072]{1,0:T(8,128)} async-done(((f32[768,3072]{1,0:T(8,128)}), f32[768,3072]{1,0:T(8,128)}) %all-reduce.12.cloned.1.call-update) | async-done | bytes 9437200
  1059.9 1.6 constant_dynamic-slice_fusion
  (47 shorter events, 4.4 us)
Async XLA Ops:
  7.2 0.9 copy-start
  10.7 15.8 %all-to-all-start.2 = ((bf16[4,32,768]{2,0,1:T(4,128)(2,1)}), bf16[4,32,768]{2,0,1:T(4,128)(2,1)S(1)}, u32[]{:S(2)}, u32[]{:S(2)}) async-start(bf16[4,32,768]{2,0,1:T(4,128)(2,1)} %copy.37), calls=%async_computation.2 | async-start | bytes 393216 | tf_op jit(solution)/shard_map/all_to_all | solution.py:120
  26.6 13.9 %all-to-all-start.3 = ((bf16[4,32,768]{2,0,1:T(4,128)(2,1)}), bf16[4,32,768]{2,0,1:T(4,128)(2,1)S(1)}, u32[]{:S(2)}, u32[]{:S(2)}) async-start(bf16[4,32,768]{2,0,1:T(4,128)(2,1)} %copy.38), calls=%async_computation.3 | async-start | bytes 393216 | tf_op jit(solution)/shard_map/all_to_all | solution.py:117
  40.5 13.5 %all-to-all-start = ((bf16[4,32,768]{2,0,1:T(4,128)(2,1)}), bf16[4,32,768]{2,0,1:T(4,128)(2,1)S(1)}, u32[]{:S(2)}, u32[]{:S(2)}) async-start(bf16[4,32,768]{2,0,1:T(4,128)(2,1)} %copy.33), calls=%async_computation | async-start | bytes 393216 | tf_op jit(solution)/shard_map/all_to_all | solution.py:116
  46.2 119.1 %all-reduce.8.cloned.1.call-start = ((), (), s32[]{:S(2)}) async-start(), calls=%async_computation.9 | async-start | bytes 1572864 | tf_op jit(solution)/shard_map/psum | solution.py:57
  48.2 117.2 %copy-start.3 = (s32[128]{0:T(128)S(1)}, s32[128]{0:T(128)}, u32[]{:S(2)}) copy-start(s32[128]{0:T(128)} %param.9) | copy-start | bytes 1540
  48.2 117.2 %copy-start.4 = (s32[128]{0:T(128)S(1)}, s32[128]{0:T(128)}, u32[]{:S(2)}) copy-start(s32[128]{0:T(128)} %param.8) | copy-start | bytes 1540
  54.0 16.6 %all-to-all-start.1 = ((bf16[4,32,768]{2,0,1:T(4,128)(2,1)}), bf16[4,32,768]{2,0,1:T(4,128)(2,1)S(1)}, u32[]{:S(2)}, u32[]{:S(2)}) async-start(bf16[4,32,768]{2,0,1:T(4,128)(2,1)} %copy.34), calls=%async_computation.1 | async-start | bytes 393216 | tf_op jit(solution)/shard_map/all_to_all | solution.py:115
  59.8 375.3 %all-reduce.6.cloned.1.call-start = ((), (), s32[]{:S(2)}) async-start(), calls=%async_computation.8 | async-start | bytes 1572864 | tf_op jit(solution)/shard_map/psum | solution.py:52
  72.6 629.4 %all-reduce.10.cloned.1.call-start = ((), (), s32[]{:S(2)}) async-start(), calls=%async_computation.10 | async-start | bytes 1572864 | tf_op jit(solution)/shard_map/psum | solution.py:56
  435.1 12.8 %copy-start.1 = (f32[12,128,128]{2,1,0:T(8,128)S(1)}, f32[12,128,128]{2,1,0:T(8,128)}, u32[]{:S(2)}) copy-start(f32[12,128,128]{2,1,0:T(8,128)} %all-reduce.6.cloned.1.call-done) | copy-start | bytes 2359300
  440.4 263.2 %all-to-all-start.6 = ((bf16[32,2,1536]{2,1,0:T(2,128)(2,1)}), bf16[32,2,1536]{2,1,0:T(2,128)(2,1)S(1)}, u32[]{:S(2)}, u32[]{:S(2)}) async-start(bf16[32,2,1536]{2,1,0:T(2,128)(2,1)} %reshape.210), calls=%async_computation.6 | async-start | bytes 393216 | tf_op jit(solution)/shard_map/all_to_all | solution.py:131
  703.6 28.6 %all-to-all-start.7 = ((bf16[32,2,1536]{2,1,0:T(2,128)(2,1)}), bf16[32,2,1536]{2,1,0:T(2,128)(2,1)S(1)}, u32[]{:S(2)}, u32[]{:S(2)}) async-start(bf16[32,2,1536]{2,1,0:T(2,128)(2,1)} %reshape.212), calls=%async_computation.7 | async-start | bytes 393216 | tf_op jit(solution)/shard_map/all_to_all | solution.py:128
  732.2 13.5 %all-to-all-start.4 = ((bf16[32,2,1536]{2,1,0:T(2,128)(2,1)}), bf16[32,2,1536]{2,1,0:T(2,128)(2,1)S(1)}, u32[]{:S(2)}, u32[]{:S(2)}) async-start(bf16[32,2,1536]{2,1,0:T(2,128)(2,1)} %reshape.206), calls=%async_computation.4 | async-start | bytes 393216 | tf_op jit(solution)/shard_map/all_to_all | solution.py:129
  745.7 14.1 %all-to-all-start.5 = ((bf16[32,2,1536]{2,1,0:T(2,128)(2,1)}), bf16[32,2,1536]{2,1,0:T(2,128)(2,1)}, u32[]{:S(2)}, u32[]{:S(2)}) async-start(bf16[32,2,1536]{2,1,0:T(2,128)(2,1)} %reshape.208), calls=%async_computation.5 | async-start | bytes 393216 | tf_op jit(solution)/shard_map/all_to_all | solution.py:130
  752.1 307.8 %all-reduce.12.cloned.1.call-start = ((), (), s32[]{:S(2)}) async-start(), calls=%async_computation.11 | async-start | bytes 18874368
  752.8 13.4 %copy-start.2 = (bf16[4,32,768]{2,1,0:T(8,128)(2,1)S(1)}, bf16[4,32,768]{2,1,0:T(8,128)(2,1)}, u32[]{:S(2)}) copy-start(bf16[4,32,768]{2,1,0:T(8,128)(2,1)} %param.5) | copy-start | bytes 589828
Sparse Core Ops, SparseCore 0:
  49.7 115.6 all-reduce.7
  170.8 264.2 all-reduce.5
  437.7 264.1 all-reduce.9
  780.2 279.6 all-reduce.11
